TPU v7x, 32 devices: a whole 2x2x4 slice. The times are simulated.
32 devices in a mesh: group: 1, tile: 8 (over z, core), dp: 4 (over y, x).
Axes of the slice: x: 2, y: 2, z: 4, core: 2. Of those that a mesh axis runs over, the one named last changes fastest.
Arguments:
- activations: bfloat16 [4, 8, 24, 24, 128], P(('group', 'dp'), 'tile'), may hold values from -6 to 6
- cotangent: bfloat16 [4, 8, 24, 24, 128], P(('group', 'dp'), 'tile'), may hold values from -1.5 to 1.5
- kernel: bfloat16 [1152, 128], P('group'), may hold values from -0.1875 to 0.1875
- turning: int32 [8], P('tile'), may hold values from 0 to 3
- orient: int32 [8, 4], P('tile'), may hold values from 0 to 7, as said below
- left_factor: float32 [1152, 1152], P(('group', 'tile')), may hold values from -0.15 to 5.15
- left_basis: float32 [1152, 1152], P(('group', 'tile'), 'dp'), may hold values from -0.026516504 to 1.0265165
- right_factor: float32 [128, 128], P('group'), may hold values from -4.26 to 49.26
- right_basis: float32 [128, 128], P('group'), may hold values from -0.079549513 to 1.0795495
- momentum: float32 [1152, 128], P(('group', 'dp')), may hold values from -1.5 to 1.5
- second_moment: float32 [1152, 128], P(('group', 'dp')), may hold values from 0.02 to 0.2
Outputs:
- output: bfloat16 [4, 8, 24, 24, 128], P(('group', 'dp'), 'tile')
- input_grad: bfloat16 [4, 8, 24, 24, 128], P(('group', 'dp'), 'tile')
- kernel_grad: float32 [1152, 128], P('group')
- left_factor_new: float32 [1152, 1152], P(('group', 'tile'))
- left_basis_new: float32 [1152, 1152], P(('group', 'tile'))
- right_factor_new: float32 [128, 128], P('group')
- right_basis_new: float32 [128, 128], P('group')
- momentum_new: float32 [1152, 128], P(('group', 'dp'))
- second_new: float32 [1152, 128], P(('group', 'dp'))
- update: float32 [1152, 128], P(('group', 'tile'))
Inputs may be any that keep to these rules, and one draw needn't show every extreme that they name: 0 where edge e of tile t leaves the patch; otherwise orient[t, e] % 4 is the edge of neighbor[t, e] that heads back to t, and 4 is added where the two edges' cell orders run opposite ways.
All inputs are finite; a program needn't handle non-finite values.
Results may differ from a plain program's by a relative error of at most 0.0025.
Values may be sent and summed in bfloat16 or wider, within the bound.
A program may use at most 128 MiB of HBM per device.

v0:
```python
import math
import jax
import jax.numpy as jnp
from jax import lax
from jax.sharding import PartitionSpec as P

highest = lax.Precision.HIGHEST
epsilon = 1e-08


def edge_strips(values):
    return jnp.stack(
        [values[..., 0, :, :], values[..., :, -1, :], values[..., -1, :, :], values[..., :, 0, :]],
        axis=0,
    )


def cycle_strips(spread):
    return jnp.stack(
        [spread[:, 0, 1:-1], spread[:, 1:-1, -1], spread[:, -1, 1:-1], spread[:, 1:-1, 0]], axis=0
    )


def assemble(tile_vals, borders):
    middle = jnp.concatenate(
        [borders[3][:, :, None, :], tile_vals, borders[1][:, :, None, :]], axis=2
    )
    top_row = jnp.pad(borders[0], ((0, 0), (1, 1), (0, 0)))[:, None]
    bottom_row = jnp.pad(borders[2], ((0, 0), (1, 1), (0, 0)))[:, None]
    return jnp.concatenate([top_row, middle, bottom_row], axis=1)


def tap_patches(padded, side):
    pieces = [
        padded[:, row_off : row_off + side, col_off : col_off + side, :]
        for row_off in range(3)
        for col_off in range(3)
    ]
    joined = jnp.concatenate(pieces, axis=-1)
    return joined.reshape(-1, joined.shape[-1])


def spread_back(flat_grads, kernel, sample_count, side):
    channels = kernel.shape[1]
    summed = jnp.zeros((sample_count, side + 2, side + 2, channels), jnp.float32)
    for tap_index in range(9):
        row_off, col_off = divmod(tap_index, 3)
        weight_tap = kernel[tap_index * channels : (tap_index + 1) * channels]
        contrib = lax.dot_general(
            flat_grads, weight_tap, (((1,), (1,)), ((), ())), preferred_element_type=jnp.float32
        )
        contrib = contrib.reshape(sample_count, side, side, channels)
        summed = summed + jnp.pad(
            contrib, ((0, 0), (row_off, 2 - row_off), (col_off, 2 - col_off), (0, 0))
        )
    return summed


def absorb_rims(interior, incoming):
    result = interior.at[..., 0, :, :].add(incoming[0])
    result = result.at[..., :, -1, :].add(incoming[1])
    result = result.at[..., -1, :, :].add(incoming[2])
    return result.at[..., :, 0, :].add(incoming[3])


def flip_edges(strips, flipped):
    return jnp.where(flipped[:, None, None, None], strips[:, :, ::-1, :], strips)


def pick_gathered(everything, near_tiles, facing, flipped, usable):
    flat = everything.reshape(everything.shape[0] * 4, -1)
    wanted = jnp.where(usable, near_tiles * 4 + facing, -1)
    selector = (lax.broadcasted_iota(jnp.int32, (4, flat.shape[0]), 1) == wanted[:, None]).astype(
        jnp.bfloat16
    )
    picked = jnp.dot(selector, flat, preferred_element_type=jnp.float32).astype(jnp.bfloat16)
    return flip_edges(picked.reshape((4,) + everything.shape[2:]), flipped)


def orthonormal(power):
    gram = lax.dot_general(power, power, (((0,), (0,)), ((), ())), precision=highest)
    lower = jnp.linalg.cholesky(gram)
    return lax.linalg.triangular_solve(lower, power.T, left_side=True, lower=True).T


def body(
    activations,
    cotangent,
    kernel,
    turning,
    orient,
    left_factor,
    left_basis,
    right_factor,
    right_basis,
    momentum,
    second_moment,
):
    tiles = lax.axis_size("tile")
    dp_count = lax.axis_size("dp")
    tile_index = lax.axis_index("tile")
    dp_index = lax.axis_index("dp")
    tile_vals = activations[:, 0]
    tile_grads = cotangent[:, 0]
    sample_count = tile_vals.shape[0]
    side = tile_vals.shape[1]
    channels = tile_vals.shape[-1]
    own_turn = turning[0]
    facing = orient[0] % 4
    flipped = orient[0] >= 4
    heading = (jnp.arange(4, dtype=jnp.int32) + own_turn) % 4
    row_of = tile_index // 4
    col_of = tile_index % 4
    room = jnp.stack([row_of > 0, col_of < 3, row_of < tiles // 4 - 1, col_of > 0])
    usable = (
        jnp.sum(
            jnp.where(
                heading[:, None] == jnp.arange(4, dtype=jnp.int32)[None, :], room[None, :], False
            ),
            axis=1,
        )
        > 0
    )
    offsets = jnp.array([-4, 1, 4, -1], dtype=jnp.int32)
    near_tiles = tile_index + jnp.sum(
        jnp.where(heading[:, None] == jnp.arange(4, dtype=jnp.int32)[None, :], offsets[None, :], 0),
        axis=1,
    )
    strips = edge_strips(tile_vals)
    everything = lax.all_gather(strips[None], "tile", axis=0, tiled=True)
    borders = pick_gathered(everything, near_tiles, facing, flipped, usable)
    padded = assemble(tile_vals, borders)
    columns = tap_patches(padded, side)
    flat_grads = tile_grads.reshape(-1, channels)
    partial_grad = lax.dot_general(
        columns, flat_grads, (((0,), (0,)), ((), ())), preferred_element_type=jnp.float32
    )
    summed_grad = lax.psum(partial_grad, ("tile", "dp"))
    result = jnp.dot(columns, kernel, preferred_element_type=jnp.float32).astype(jnp.bfloat16)
    result = result.reshape(activations.shape)
    spread = spread_back(flat_grads, kernel, sample_count, side)
    rim_cells = cycle_strips(spread).astype(jnp.bfloat16)
    all_rims = lax.all_gather(rim_cells[None], "tile", axis=0, tiled=True)
    incoming = pick_gathered(all_rims, near_tiles, facing, flipped, usable)
    input_grad = absorb_rims(spread[:, 1:-1, 1:-1], incoming.astype(jnp.float32)).astype(
        jnp.bfloat16
    )
    input_grad = input_grad.reshape(cotangent.shape)
    cells = dp_count * sample_count * tiles * side * side
    grad = summed_grad * (1.0 / math.sqrt(cells))
    rows_per = left_factor.shape[0]
    width = left_factor.shape[1]
    cols_per = left_basis.shape[1]
    col_start = dp_index * cols_per
    grad_rows = lax.dynamic_slice_in_dim(grad, tile_index * rows_per, rows_per, 0)
    left_new = 0.95 * left_factor + 0.05 * lax.dot_general(
        grad_rows, grad, (((1,), (1,)), ((), ())), precision=highest
    )
    basis_rows = lax.all_gather(left_basis, "dp", axis=1, tiled=True)
    power = jnp.zeros((rows_per, width), jnp.float32) + jnp.dot(
        left_new,
        lax.all_gather(basis_rows.astype(jnp.bfloat16), "tile", axis=0, tiled=True).astype(
            jnp.float32
        ),
        precision=highest,
    )
    power_cols = lax.dynamic_slice_in_dim(power, col_start, cols_per, 1)
    gram_part = lax.psum(
        lax.dot_general(power, power_cols, (((0,), (0,)), ((), ())), precision=highest), "tile"
    )
    gram = lax.all_gather(gram_part, "dp", axis=1, tiled=True)
    lower = jnp.linalg.cholesky(gram)
    basis_new = lax.linalg.triangular_solve(lower, power.T, left_side=True, lower=True).T
    right_new = 0.95 * right_factor + 0.05 * lax.dot_general(
        grad, grad, (((0,), (0,)), ((), ())), precision=highest
    )
    right_basis_new = orthonormal(jnp.dot(right_new, right_basis, precision=highest))
    back = lax.psum(jnp.dot(left_basis, momentum, precision=highest), "dp")
    basis_cols = lax.dynamic_slice_in_dim(basis_new, col_start, cols_per, 1)
    turned_momentum, turned_grad = lax.psum(
        (
            lax.dot_general(basis_cols, back, (((0,), (0,)), ((), ())), precision=highest),
            lax.dot_general(basis_cols, grad_rows, (((0,), (0,)), ((), ())), precision=highest),
        ),
        "tile",
    )
    right_turn = lax.dot_general(
        right_basis, right_basis_new, (((0,), (0,)), ((), ())), precision=highest
    )
    rotated = jnp.dot(turned_momentum, right_turn, precision=highest)
    projected = jnp.dot(turned_grad, right_basis_new, precision=highest)
    momentum_new = 0.9 * rotated + 0.1 * projected
    second_new = 0.95 * second_moment + 0.05 * projected * projected
    normalized = momentum_new / (jnp.sqrt(second_new) + epsilon)
    whole_moment = lax.all_gather(normalized, "dp", axis=0, tiled=True)
    update_rows = jnp.dot(basis_new, whole_moment, precision=highest)
    update = lax.dot_general(
        update_rows, right_basis_new, (((1,), (1,)), ((), ())), precision=highest
    )
    return (
        result,
        input_grad,
        grad,
        left_new,
        basis_new,
        right_new,
        right_basis_new,
        momentum_new,
        second_new,
        update,
    )


def solution(mesh):
    placed = (
        P(("group", "dp"), "tile", None, None, None),
        P(("group", "dp"), "tile", None, None, None),
        P("group", None),
        P("tile"),
        P("tile", None),
        P(("group", "tile"), None),
        P(("group", "tile"), "dp"),
        P("group", None),
        P("group", None),
        P(("group", "dp"), None),
        P(("group", "dp"), None),
    )
    return jax.shard_map(
        body,
        mesh=mesh,
        in_specs=placed,
        out_specs=(
            P(("group", "dp"), "tile", None, None, None),
            P(("group", "dp"), "tile", None, None, None),
            P("group", None),
            P(("group", "tile"), None),
            P(("group", "tile"), None),
            P("group", None),
            P("group", None),
            P(("group", "dp"), None),
            P(("group", "dp"), None),
            P(("group", "tile"), None),
        ),
        check_vma=False,
    )
```

profile of v0, /device:TPU:0, one launch (start us, length us, event | category | flops | bytes accessed | tf_op | source)
XLA Modules:
  0.0 795.9 jit_solution(18225096363000132094)
XLA Ops:
  19.2 15.8 %all_gather.19 = bf16[8,4,1,24,128]{4,3,2,1,0:T(8,128)(2,1)S(1)} all-gather(bf16[1,4,1,24,128]{4,3,2,1,0:T(8,128)(2,1)S(1)} %pad_maximum_fusion.4), channel_id=1, replica_groups=mesh['group'=1,'tile'=8,'dp'=4] {'tile'}, dimensions={0}, use_global_device_ids=true | all-gather | bytes 221184 | tf_op jit(solution)/shard_map/all_gather | solution.py:143
  36.3 14.1 %all-gather = bf16[32,1,24,128]{3,2,1,0:T(8,128)(2,1)S(1)} all-gather(bf16[4,1,24,128]{3,2,1,0:T(8,128)(2,1)S(1)} %pad_maximum_fusion.3), channel_id=2, replica_groups=mesh['group'=1,'tile'=8,'dp'=4] {'tile'}, dimensions={0}, use_global_device_ids=true | all-gather | bytes 221184 | tf_op jit(solution)/shard_map/all_gather | solution.py:130
  53.1 10.2 %all-gather.1 = bf16[4,288,144]{1,2,0:T(8,128)(2,1)S(1)} all-gather(bf16[1,288,144]{1,2,0:T(8,128)(2,1)S(1)} %bitcast_convert_fusion), channel_id=1, replica_groups=mesh['group'=1,'tile'=8,'dp'=4] {'dp'}, dimensions={0}, use_global_device_ids=true | all-gather | bytes 414720 | tf_op jit(solution)/shard_map/all_gather | solution.py:159
  64.7 132.0 %all-reduce.18.cloned.1.call-done = f32[1152,128]{1,0:T(8,128)} async-done(((f32[1152,128]{1,0:T(8,128)}), f32[1152,128]{1,0:T(8,128)}) %all-reduce.18.cloned.1.call-update) | async-done | bytes 589840 | tf_op jit(solution)/shard_map/psum | solution.py:138
  199.9 3.6 fusion.152
  203.5 2.6 fusion.52
  206.1 60.6 %all-reduce.20.cloned.1.call-done = f32[1152,288]{0,1:T(8,128)} async-done(((f32[1152,288]{0,1:T(8,128)}), f32[1152,288]{0,1:T(8,128)}) %all-reduce.20.cloned.1.call-update) | async-done | bytes 1327120 | tf_op jit(solution)/shard_map/psum | solution.py:168
  276.5 11.7 %cholesky.693 = f32[128,128]{1,0:T(8,128)S(1)} custom-call(f32[128,128]{1,0:T(8,128)S(1)} %fusion.98), custom_call_target="Cholesky" | custom-call | tf_op jit(solution)/shard_map/jit(cholesky)/cholesky | solution.py:82
  289.6 9.8 %custom-call.85 = f32[1,128,128]{1,2,0:T(8,128)S(1)} custom-call(f32[1,128,128]{2,1,0:T(8,128)S(1)} %fusion.85), custom_call_target="InvertDiagBlocksLowerTriangular" | custom-call | tf_op jit(solution)/shard_map/triangular_solve | solution.py:83
  300.4 28.1 %all-gather.7.cloned.1.call-done = f32[1152,1152]{0,1:T(8,128)} async-done(((f32[1152,288]{0,1:T(8,128)}), f32[1152,1152]{0,1:T(8,128)}) %all-gather.7.cloned.1.call-update) | async-done | bytes 5308432 | tf_op jit(solution)/shard_map/all_gather | solution.py:171
  328.5 7.2 copy.93
  335.7 4.7 fusion
  342.7 11.7 %cholesky.273 = f32[128,128]{1,0:T(8,128)S(1)} custom-call(f32[128,128]{1,0:T(8,128)S(1)} %cholesky.705), custom_call_target="Cholesky" | custom-call | tf_op jit(solution)/shard_map/jit(cholesky)/cholesky | solution.py:172
  354.4 2.7 cholesky.303
  357.1 9.8 %custom-call.76 = f32[1,128,128]{1,2,0:T(8,128)S(1)} custom-call(f32[1,128,128]{2,1,0:T(8,128)S(1)} %get-tuple-element.210), custom_call_target="InvertDiagBlocksLowerTriangular" | custom-call | tf_op jit(solution)/shard_map/jit(cholesky)/cholesky | solution.py:172
  371.1 11.7 %cholesky.294 = f32[128,128]{1,0:T(8,128)S(1)} custom-call(f32[128,128]{1,0:T(8,128)S(1)} %cholesky.709), custom_call_target="Cholesky" | custom-call | tf_op jit(solution)/shard_map/jit(cholesky)/cholesky | solution.py:172
  383.5 10.0 %custom-call.77 = f32[1,128,128]{1,2,0:T(8,128)S(1)} custom-call(f32[1,128,128]{2,1,0:T(8,128)S(1)} %get-tuple-element.207), custom_call_target="InvertDiagBlocksLowerTriangular" | custom-call | tf_op jit(solution)/shard_map/jit(cholesky)/cholesky | solution.py:172
  397.1 11.7 %cholesky.321 = f32[128,128]{1,0:T(8,128)S(1)} custom-call(f32[128,128]{1,0:T(8,128)S(1)} %cholesky.714), custom_call_target="Cholesky" | custom-call | tf_op jit(solution)/shard_map/jit(cholesky)/cholesky | solution.py:172
  409.4 9.8 %custom-call.78 = f32[1,128,128]{1,2,0:T(8,128)S(1)} custom-call(f32[1,128,128]{2,1,0:T(8,128)S(1)} %get-tuple-element.204), custom_call_target="InvertDiagBlocksLowerTriangular" | custom-call | tf_op jit(solution)/shard_map/jit(cholesky)/cholesky | solution.py:172
  420.5 2.6 convolution_subtract_fusion.2
  423.2 11.9 %cholesky.583 = f32[128,128]{1,0:T(8,128)S(1)} custom-call(f32[128,128]{1,0:T(8,128)S(1)} %cholesky.719), custom_call_target="Cholesky" | custom-call | tf_op jit(solution)/shard_map/jit(cholesky)/cholesky | solution.py:172
  435.7 9.8 %custom-call.79 = f32[1,128,128]{1,2,0:T(8,128)S(1)} custom-call(f32[1,128,128]{2,1,0:T(8,128)S(1)} %get-tuple-element.201), custom_call_target="InvertDiagBlocksLowerTriangular" | custom-call | tf_op jit(solution)/shard_map/jit(cholesky)/cholesky | solution.py:172
  446.7 2.6 fusion.6
  449.3 11.7 %cholesky.602 = f32[128,128]{1,0:T(8,128)S(1)} custom-call(f32[128,128]{1,0:T(8,128)S(1)} %cholesky.724), custom_call_target="Cholesky" | custom-call | tf_op jit(solution)/shard_map/jit(cholesky)/cholesky | solution.py:172
  461.7 10.2 %custom-call.80 = f32[1,128,128]{1,2,0:T(8,128)S(1)} custom-call(f32[1,128,128]{2,1,0:T(8,128)S(1)} %get-tuple-element.198), custom_call_target="InvertDiagBlocksLowerTriangular" | custom-call | tf_op jit(solution)/shard_map/jit(cholesky)/cholesky | solution.py:172
  473.0 2.8 fusion.12
  475.8 11.7 %cholesky.622 = f32[128,128]{1,0:T(8,128)S(1)} custom-call(f32[128,128]{1,0:T(8,128)S(1)} %cholesky.729), custom_call_target="Cholesky" | custom-call | tf_op jit(solution)/shard_map/jit(cholesky)/cholesky | solution.py:172
  488.2 9.8 %custom-call.81 = f32[1,128,128]{1,2,0:T(8,128)S(1)} custom-call(f32[1,128,128]{2,1,0:T(8,128)S(1)} %get-tuple-element.195), custom_call_target="InvertDiagBlocksLowerTriangular" | custom-call | tf_op jit(solution)/shard_map/jit(cholesky)/cholesky | solution.py:172
  499.0 2.6 fusion.15
  501.6 11.9 %cholesky.642 = f32[128,128]{1,0:T(8,128)S(1)} custom-call(f32[128,128]{1,0:T(8,128)S(1)} %cholesky.734), custom_call_target="Cholesky" | custom-call | tf_op jit(solution)/shard_map/jit(cholesky)/cholesky | solution.py:172
  514.1 9.8 %custom-call.82 = f32[1,128,128]{1,2,0:T(8,128)S(1)} custom-call(f32[1,128,128]{2,1,0:T(8,128)S(1)} %get-tuple-element.192), custom_call_target="InvertDiagBlocksLowerTriangular" | custom-call | tf_op jit(solution)/shard_map/jit(cholesky)/cholesky | solution.py:172
  527.1 11.7 %cholesky.662 = f32[128,128]{1,0:T(8,128)S(1)} custom-call(f32[128,128]{1,0:T(8,128)S(1)} %cholesky.739), custom_call_target="Cholesky" | custom-call | tf_op jit(solution)/shard_map/jit(cholesky)/cholesky | solution.py:172
  539.5 9.8 %custom-call.83 = f32[1,128,128]{1,2,0:T(8,128)S(1)} custom-call(f32[1,128,128]{2,1,0:T(8,128)S(1)} %get-tuple-element.189), custom_call_target="InvertDiagBlocksLowerTriangular" | custom-call | tf_op jit(solution)/shard_map/jit(cholesky)/cholesky | solution.py:172
  551.9 11.9 %cholesky.680 = f32[128,128]{1,0:T(8,128)S(1)} custom-call(f32[128,128]{1,0:T(8,128)S(1)} %convolution_subtract_fusion.12), custom_call_target="Cholesky" | custom-call | tf_op jit(solution)/shard_map/jit(cholesky)/cholesky | solution.py:172
  576.1 5.2 select_select_fusion
  581.3 31.4 %while.5 = (s32[]{:T(128)}, f32[1152,1152]{1,0:T(8,128)}, s32[9,2]{0,1:T(2,128)S(1)}, f32[9,128,128]{2,1,0:T(8,128)}, s32[]{:T(128)}) while((s32[]{:T(128)}, f32[1152,1152]{1,0:T(8,128)}, s32[9,2]{0,1:T(2,128)S(1)}, f32[9,128,128]{2,1,0:T(8,128)}, s32[]{:T(128)}) %tuple.112), condition=%wide.while_cond.4, body=%wide.while_body.4.sunk | while | flops 2 | bytes 132205 | solution.py:173
  581.9 2.9 bitcast_dynamic-update-slice_fusion.2
  585.4 2.9 bitcast_dynamic-update-slice_fusion.2
  588.9 2.9 bitcast_dynamic-update-slice_fusion.2
  592.4 2.9 bitcast_dynamic-update-slice_fusion.2
  595.9 2.9 bitcast_dynamic-update-slice_fusion.2
  599.4 2.9 bitcast_dynamic-update-slice_fusion.2
  603.0 2.9 bitcast_dynamic-update-slice_fusion.2
  606.5 2.9 bitcast_dynamic-update-slice_fusion.2
  610.0 2.8 bitcast_dynamic-update-slice_fusion.2
  612.8 89.2 %custom-call.84 = f32[9,128,128]{1,2,0:T(8,128)S(1)} custom-call(f32[9,128,128]{2,1,0:T(8,128)} %get-tuple-element.65), custom_call_target="InvertDiagBlocksLowerTriangular" | custom-call | tf_op jit(solution)/shard_map/triangular_solve | solution.py:173
  719.5 52.8 %all-reduce.24.cloned.1.call-done = (f32[288,128]{1,0:T(8,128)}, f32[288,128]{1,0:T(8,128)}) async-done(((f32[288,128]{1,0:T(8,128)}, f32[288,128]{1,0:T(8,128)}), (f32[288,128]{1,0:T(8,128)}, f32[288,128]{1,0:T(8,128)})) %all-reduce.24.cloned.1.call-update) | async-done | bytes 294928 | tf_op jit(solution)/shard_map/psum | solution.py:180
  775.4 11.2 %all_gather.23 = f32[1152,128]{1,0:T(8,128)S(1)} all-gather(f32[288,128]{1,0:T(8,128)S(1)} %get-tuple-element.128), channel_id=1, replica_groups=mesh['group'=1,'tile'=8,'dp'=4] {'dp'}, dimensions={0}, use_global_device_ids=true | all-gather | bytes 737280 | tf_op jit(solution)/shard_map/all_gather | solution.py:195
  (197 shorter events, 90.1 us)
Async XLA Ops:
  8.0 1.0 copy-start
  8.0 27.8 %copy-start.11 = (s32[4]{0:T(128)S(1)}, s32[4]{0:T(128)}, u32[]{:S(2)}) copy-start(s32[4]{0:T(128)} %constant.530.clone) | copy-start | bytes 52
  8.0 11.1 %copy-start.5 = (bf16[1,1,24,24,128]{4,3,2,1,0:T(8,128)(2,1)S(1)}, bf16[1,1,24,24,128]{4,3,2,1,0:T(8,128)(2,1)}, u32[]{:S(2)}) copy-start(bf16[1,1,24,24,128]{4,3,2,1,0:T(8,128)(2,1)} %param.20) | copy-start | bytes 442372
  8.0 27.6 %copy-start.10 = (s32[1,4]{1,0:T(1,128)S(1)}, s32[1,4]{1,0:T(1,128)}, u32[]{:S(2)}) copy-start(s32[1,4]{1,0:T(1,128)} %param.24) | copy-start | bytes 52
  8.1 188.6 %all-reduce.18.cloned.1.call-start = ((), (), s32[]{:S(2)}) async-start(), calls=%async_computation | async-start | bytes 1179648 | tf_op jit(solution)/shard_map/psum | solution.py:138
  19.0 34.1 %copy-start.6 = (f32[144,288]{1,0:T(8,128)S(1)}, f32[144,288]{1,0:T(8,128)}, u32[]{:S(2)}) copy-start(f32[144,288]{1,0:T(8,128)} %param.26) | copy-start | bytes 497668
  53.1 146.8 %all-gather.5.cloned.1.call-start = ((), (), s32[]{:S(2)}) async-start(), calls=%async_computation.1 | async-start | bytes 2985984 | tf_op jit(solution)/shard_map/all_gather | solution.py:162
  64.6 202.1 %all-reduce.20.cloned.1.call-start = ((), (), s32[]{:S(2)}) async-start(), calls=%async_computation.2 | async-start | bytes 2654208 | tf_op jit(solution)/shard_map/psum | solution.py:168
  197.8 517.7 %copy-start.2 = (f32[1152,128]{1,0:T(8,128)}, f32[1152,128]{1,0:T(8,128)S(1)}, u32[]{:S(2)}) copy-start(f32[1152,128]{1,0:T(8,128)S(1)} %broadcast_multiply_fusion) | copy-start | bytes 1769476
  199.8 71.1 %copy-start.3 = (f32[144,1152]{1,0:T(8,128)}, f32[144,1152]{1,0:T(8,128)S(1)}, u32[]{:S(2)}) copy-start(f32[144,1152]{1,0:T(8,128)S(1)} %fusion.1) | copy-start | bytes 1990660
  203.4 72.4 %copy-start.7 = (f32[128,128]{1,0:T(8,128)S(1)}, f32[128,128]{1,0:T(8,128)}, u32[]{:S(2)}) copy-start(f32[128,128]{1,0:T(8,128)} %param.28) | copy-start | bytes 196612
  206.0 122.4 %all-gather.7.cloned.1.call-start = ((), (), s32[]{:S(2)}) async-start(), calls=%async_computation.3 | async-start | bytes 6635520 | tf_op jit(solution)/shard_map/all_gather | solution.py:171
  266.7 450.2 %all-reduce.22.cloned.1.call-start = ((), (), s32[]{:S(2)}) async-start(), calls=%async_computation.4 | async-start | bytes 147456 | tf_op jit(solution)/shard_map/psum | solution.py:178
  268.7 503.5 %all-reduce.24.cloned.1.call-start = ((), (), s32[]{:S(2)}) async-start(), calls=%async_computation.5 | async-start | bytes 589824 | tf_op jit(solution)/shard_map/psum | solution.py:180
  275.9 59.8 %copy-start.8 = (f32[128,128]{1,0:T(8,128)}, f32[128,128]{1,0:T(8,128)S(1)}, u32[]{:S(2)}) copy-start(f32[128,128]{1,0:T(8,128)S(1)} %fusion.19) | copy-start | bytes 196612
  340.4 2.3 copy-start.1
  703.6 69.9 %copy-start.9 = (f32[288,128]{1,0:T(8,128)S(1)}, f32[288,128]{1,0:T(8,128)}, u32[]{:S(2)}) copy-start(f32[288,128]{1,0:T(8,128)} %param.30) | copy-start | bytes 442372
  715.4 72.7 %copy-start.4 = (f32[1152,144]{0,1:T(8,128)}, f32[1152,144]{0,1:T(8,128)S(1)}, u32[]{:S(2)}) copy-start(f32[1152,144]{0,1:T(8,128)S(1)} %convolution_dynamic-update-slice_fusion.6) | copy-start | bytes 1990660
Sparse Core Ops, SparseCore 0:
  53.2 143.4 all-reduce.17
  266.8 61.6 all-gather.6
  331.9 40.6 all-reduce.21
Sparse Core Ops, SparseCore 1:
  64.7 35.0 all-gather.4
  206.1 60.5 all-reduce.19
  719.4 52.8 all-reduce.23
where the time goes:
time: 806 us; the launch traced here: 796 us
  other arithmetic  322 us (40%)
  waiting for transfers between devices  273 us (34%)
  matrix products  76.5 us (9%)
  blocking collectives  51.3 us (6%)
  local copies, waits for them, and re-layouts  49.5 us (6%)
  between operations  23.1 us (3%)
    another operation x35, other arithmetic, body(): lower = jnp.linalg.cholesky(gram)  196 us
    psum x1, waiting for transfers between devices, body(): summed_grad = lax.psum(partial_grad, ('tile', 'dp'))  132 us
    another operation x3, other arithmetic, body(): lax.linalg.triangular_solve(lower, power.T, left_side=True, lower=True)  94.4 us
    psum x1, waiting for transfers between devices, body(): lax.psum(lax.dot_general(power, power_cols, (((0,), (0,)), ((), ())), pre...  60.6 us
    psum x1, waiting for transfers between devices, body(): lax.psum((lax.dot_general(basis_cols, back, (((0,), (0,)), ((), ())), pre...  52.8 us
    another operation x27, local copies, waits for them, and re-layouts  31.4 us
    another operation x16, matrix products, body(): lower = jnp.linalg.cholesky(gram)  28.7 us
    all_gather x1, waiting for transfers between devices, body(): gram = lax.all_gather(gram_part, 'dp', axis=1, tiled=True)  28.1 us
  transfers between devices with their start and end apart: 6, of which 4 were waited for; matrix products, arithmetic and copies ran while one was open for 53% of the time, Pallas kernels for 0%

commit v1 on v0

--- a/solution.py
+++ b/solution.py
@@ -6,6 +6,18 @@
 
 highest = lax.Precision.HIGHEST
 epsilon = 1e-08
+
+
+def doubled_up(array, axis, dim):
+    ways, here, step = (lax.axis_size(axis), lax.axis_index(axis), array.shape[dim])
+    line, have = (array, 1)
+    while have < ways:
+        line = jnp.concatenate(
+            [line, lax.ppermute(line, axis, [(d, (d - have) % ways) for d in range(ways)])],
+            axis=dim,
+        )
+        have = 2 * have
+    return jnp.roll(line, here * step, axis=dim)
 
 
 def edge_strips(values):
@@ -168,7 +180,7 @@
     gram_part = lax.psum(
         lax.dot_general(power, power_cols, (((0,), (0,)), ((), ())), precision=highest), "tile"
     )
-    gram = lax.all_gather(gram_part, "dp", axis=1, tiled=True)
+    gram = doubled_up(gram_part, "dp", 1)
     lower = jnp.linalg.cholesky(gram)
     basis_new = lax.linalg.triangular_solve(lower, power.T, left_side=True, lower=True).T
     right_new = 0.95 * right_factor + 0.05 * lax.dot_general(

time: 806 us -> 856 us (1.062)
  local copies, waits for them, and re-layouts: 49.5 us -> 65.2 us
  waiting for transfers between devices: 273 us -> 287 us
  other arithmetic: 322 us -> 332 us
    ppermute x0 -> x2, waiting for transfers between devices: none -> 41.6 us  [doubled_up(): lax.ppermute(line, axis, [(d, (d - have) % ways) for d in range(ways)])]
    all_gather x1 -> x0, waiting for transfers between devices: 28.1 us -> none  [body(): gram = lax.all_gather(gram_part, 'dp', axis=1, tiled=True)]
    dynamic_slice x0 -> x2, local copies, waits for them, and re-layouts: none -> 9.75 us  [doubled_up(): return jnp.roll(line, here * step, axis=dim)]
    unnamed x38 -> x61, local copies, waits for them, and re-layouts: 5.06 us -> 14 us
  transfers between devices with their start and end apart: 6 -> 7, of which waited for: 4 -> 5; matrix products, arithmetic and copies ran while one was open for 53% -> 53% of each run, Pallas kernels for 0% -> 0%
where the time goes in v1:
time: 856 us; the launch traced here: 846 us
  other arithmetic  332 us (39%)
  waiting for transfers between devices  287 us (34%)
  matrix products  82 us (10%)
  local copies, waits for them, and re-layouts  65.2 us (8%)
  blocking collectives  51.4 us (6%)
  between operations  23.2 us (3%)
    another operation x35, other arithmetic, body(): lower = jnp.linalg.cholesky(gram)  196 us
    psum x1, waiting for transfers between devices, body(): summed_grad = lax.psum(partial_grad, ('tile', 'dp'))  132 us
    another operation x3, other arithmetic, body(): lax.linalg.triangular_solve(lower, power.T, left_side=True, lower=True)  95.3 us
    psum x1, waiting for transfers between devices, body(): lax.psum(lax.dot_general(power, power_cols, (((0,), (0,)), ((), ())), pre...  60.5 us
    psum x1, waiting for transfers between devices, body(): lax.psum((lax.dot_general(basis_cols, back, (((0,), (0,)), ((), ())), pre...  52.6 us
    ppermute x2, waiting for transfers between devices, doubled_up(): lax.ppermute(line, axis, [(d, (d - have) % ways) for d in range(ways)])  41.6 us
    another operation x27, local copies, waits for them, and re-layouts  31.3 us
    another operation x16, matrix products, body(): lower = jnp.linalg.cholesky(gram)  28.6 us
  transfers between devices with their start and end apart: 7, of which 5 were waited for; matrix products, arithmetic and copies ran while one was open for 53% of the time, Pallas kernels for 0%

profile of v1, /device:TPU:0, one launch (start us, length us, event | category | flops | bytes accessed | tf_op | source)
XLA Modules:
  0.0 845.7 jit_solution(15314197944084715196)
XLA Ops:
  18.5 15.9 %all_gather.16 = bf16[8,4,1,24,128]{4,3,2,1,0:T(8,128)(2,1)S(1)} all-gather(bf16[1,4,1,24,128]{4,3,2,1,0:T(8,128)(2,1)S(1)} %pad_maximum_fusion.5), channel_id=1, replica_groups=mesh['group'=1,'tile'=8,'dp'=4] {'tile'}, dimensions={0}, use_global_device_ids=true | all-gather | bytes 221184 | tf_op jit(solution)/shard_map/all_gather | solution.py:155
  35.7 14.1 %all-gather = bf16[32,1,24,128]{3,2,1,0:T(8,128)(2,1)S(1)} all-gather(bf16[4,1,24,128]{3,2,1,0:T(8,128)(2,1)S(1)} %pad_maximum_fusion.4), channel_id=2, replica_groups=mesh['group'=1,'tile'=8,'dp'=4] {'tile'}, dimensions={0}, use_global_device_ids=true | all-gather | bytes 221184 | tf_op jit(solution)/shard_map/all_gather | solution.py:142
  53.7 10.3 %all-gather.1 = bf16[4,288,144]{1,2,0:T(8,128)(2,1)S(1)} all-gather(bf16[1,288,144]{1,2,0:T(8,128)(2,1)S(1)} %bitcast_convert_fusion), channel_id=1, replica_groups=mesh['group'=1,'tile'=8,'dp'=4] {'dp'}, dimensions={0}, use_global_device_ids=true | all-gather | bytes 414720 | tf_op jit(solution)/shard_map/all_gather | solution.py:171
  65.2 132.2 %all-reduce.18.cloned.1.call-done = f32[1152,128]{1,0:T(8,128)} async-done(((f32[1152,128]{1,0:T(8,128)}), f32[1152,128]{1,0:T(8,128)}) %all-reduce.18.cloned.1.call-update) | async-done | bytes 589840 | tf_op jit(solution)/shard_map/psum | solution.py:150
  199.4 3.5 fusion.162
  206.4 60.5 %all-reduce.20.cloned.1.call-done = f32[1152,288]{0,1:T(8,128)} async-done(((f32[1152,288]{0,1:T(8,128)}), f32[1152,288]{0,1:T(8,128)}) %all-reduce.20.cloned.1.call-update) | async-done | bytes 1327120 | tf_op jit(solution)/shard_map/psum | solution.py:180
  278.8 18.7 %collective-permute-done = f32[1152,288]{0,1:T(8,128)S(1)} collective-permute-done((f32[1152,288]{0,1:T(8,128)}, f32[1152,288]{0,1:T(8,128)S(1)}, u32[]{:S(2)}, u32[]{:S(2)}) %collective-permute-start) | collective-permute-done | bytes 1327136 | tf_op jit(solution)/shard_map/ppermute | solution.py:16
  297.6 3.0 pad_maximum_fusion
  310.0 12.5 %cholesky.693 = f32[128,128]{1,0:T(8,128)S(1)} custom-call(f32[128,128]{1,0:T(8,128)} %fusion.108), custom_call_target="Cholesky" | custom-call | tf_op jit(solution)/shard_map/jit(cholesky)/cholesky | solution.py:94
  324.6 10.6 %custom-call.85 = f32[1,128,128]{1,2,0:T(8,128)S(1)} custom-call(f32[1,128,128]{2,1,0:T(8,128)} %fusion.92), custom_call_target="InvertDiagBlocksLowerTriangular" | custom-call | tf_op jit(solution)/shard_map/triangular_solve | solution.py:95
  336.4 22.8 %collective-permute-done.1 = f32[1152,576]{0,1:T(8,128)} collective-permute-done((f32[1152,576]{0,1:T(8,128)}, f32[1152,576]{0,1:T(8,128)}, u32[]{:S(2)}, u32[]{:S(2)}) %collective-permute-start.1) | collective-permute-done | bytes 2654240 | tf_op jit(solution)/shard_map/ppermute | solution.py:16
  363.3 4.0 copy-done.2
  367.3 2.7 constant_dynamic-slice_fusion.1
  370.0 7.1 copy.93
  377.1 4.8 fusion
  384.2 11.7 %cholesky.273 = f32[128,128]{1,0:T(8,128)S(1)} custom-call(f32[128,128]{1,0:T(8,128)S(1)} %cholesky.705), custom_call_target="Cholesky" | custom-call | tf_op jit(solution)/shard_map/jit(cholesky)/cholesky | solution.py:184
  395.9 2.7 cholesky.303
  398.6 9.8 %custom-call.76 = f32[1,128,128]{1,2,0:T(8,128)S(1)} custom-call(f32[1,128,128]{2,1,0:T(8,128)S(1)} %get-tuple-element.210), custom_call_target="InvertDiagBlocksLowerTriangular" | custom-call | tf_op jit(solution)/shard_map/jit(cholesky)/cholesky | solution.py:184
  412.6 11.7 %cholesky.294 = f32[128,128]{1,0:T(8,128)S(1)} custom-call(f32[128,128]{1,0:T(8,128)S(1)} %cholesky.709), custom_call_target="Cholesky" | custom-call | tf_op jit(solution)/shard_map/jit(cholesky)/cholesky | solution.py:184
  425.0 10.1 %custom-call.77 = f32[1,128,128]{1,2,0:T(8,128)S(1)} custom-call(f32[1,128,128]{2,1,0:T(8,128)S(1)} %get-tuple-element.207), custom_call_target="InvertDiagBlocksLowerTriangular" | custom-call | tf_op jit(solution)/shard_map/jit(cholesky)/cholesky | solution.py:184
  438.7 11.7 %cholesky.321 = f32[128,128]{1,0:T(8,128)S(1)} custom-call(f32[128,128]{1,0:T(8,128)S(1)} %cholesky.714), custom_call_target="Cholesky" | custom-call | tf_op jit(solution)/shard_map/jit(cholesky)/cholesky | solution.py:184
  451.1 9.8 %custom-call.78 = f32[1,128,128]{1,2,0:T(8,128)S(1)} custom-call(f32[1,128,128]{2,1,0:T(8,128)S(1)} %get-tuple-element.204), custom_call_target="InvertDiagBlocksLowerTriangular" | custom-call | tf_op jit(solution)/shard_map/jit(cholesky)/cholesky | solution.py:184
  464.7 11.9 %cholesky.583 = f32[128,128]{1,0:T(8,128)S(1)} custom-call(f32[128,128]{1,0:T(8,128)S(1)} %cholesky.719), custom_call_target="Cholesky" | custom-call | tf_op jit(solution)/shard_map/jit(cholesky)/cholesky | solution.py:184
  477.3 9.8 %custom-call.79 = f32[1,128,128]{1,2,0:T(8,128)S(1)} custom-call(f32[1,128,128]{2,1,0:T(8,128)S(1)} %get-tuple-element.201), custom_call_target="InvertDiagBlocksLowerTriangular" | custom-call | tf_op jit(solution)/shard_map/jit(cholesky)/cholesky | solution.py:184
  490.9 11.7 %cholesky.602 = f32[128,128]{1,0:T(8,128)S(1)} custom-call(f32[128,128]{1,0:T(8,128)S(1)} %cholesky.724), custom_call_target="Cholesky" | custom-call | tf_op jit(solution)/shard_map/jit(cholesky)/cholesky | solution.py:184
  503.3 10.0 %custom-call.80 = f32[1,128,128]{1,2,0:T(8,128)S(1)} custom-call(f32[1,128,128]{2,1,0:T(8,128)S(1)} %get-tuple-element.198), custom_call_target="InvertDiagBlocksLowerTriangular" | custom-call | tf_op jit(solution)/shard_map/jit(cholesky)/cholesky | solution.py:184
  514.4 2.7 slice_subtract_fusion.4
  517.1 11.7 %cholesky.622 = f32[128,128]{1,0:T(8,128)S(1)} custom-call(f32[128,128]{1,0:T(8,128)S(1)} %cholesky.729), custom_call_target="Cholesky" | custom-call | tf_op jit(solution)/shard_map/jit(cholesky)/cholesky | solution.py:184
  529.5 9.8 %custom-call.81 = f32[1,128,128]{1,2,0:T(8,128)S(1)} custom-call(f32[1,128,128]{2,1,0:T(8,128)S(1)} %get-tuple-element.195), custom_call_target="InvertDiagBlocksLowerTriangular" | custom-call | tf_op jit(solution)/shard_map/jit(cholesky)/cholesky | solution.py:184
  542.9 12.1 %cholesky.642 = f32[128,128]{1,0:T(8,128)S(1)} custom-call(f32[128,128]{1,0:T(8,128)S(1)} %cholesky.734), custom_call_target="Cholesky" | custom-call | tf_op jit(solution)/shard_map/jit(cholesky)/cholesky | solution.py:184
  555.7 9.8 %custom-call.82 = f32[1,128,128]{1,2,0:T(8,128)S(1)} custom-call(f32[1,128,128]{2,1,0:T(8,128)S(1)} %get-tuple-element.192), custom_call_target="InvertDiagBlocksLowerTriangular" | custom-call | tf_op jit(solution)/shard_map/jit(cholesky)/cholesky | solution.py:184
  568.6 11.7 %cholesky.662 = f32[128,128]{1,0:T(8,128)S(1)} custom-call(f32[128,128]{1,0:T(8,128)S(1)} %cholesky.739), custom_call_target="Cholesky" | custom-call | tf_op jit(solution)/shard_map/jit(cholesky)/cholesky | solution.py:184
  581.0 9.8 %custom-call.83 = f32[1,128,128]{1,2,0:T(8,128)S(1)} custom-call(f32[1,128,128]{2,1,0:T(8,128)S(1)} %get-tuple-element.189), custom_call_target="InvertDiagBlocksLowerTriangular" | custom-call | tf_op jit(solution)/shard_map/jit(cholesky)/cholesky | solution.py:184
  593.5 11.9 %cholesky.680 = f32[128,128]{1,0:T(8,128)S(1)} custom-call(f32[128,128]{1,0:T(8,128)S(1)} %slice_subtract_fusion.7), custom_call_target="Cholesky" | custom-call | tf_op jit(solution)/shard_map/jit(cholesky)/cholesky | solution.py:184
  617.6 5.3 select_select_fusion
  622.9 31.3 %while.5 = (s32[]{:T(128)}, f32[1152,1152]{1,0:T(8,128)}, s32[9,2]{0,1:T(2,128)S(1)}, f32[9,128,128]{2,1,0:T(8,128)}, s32[]{:T(128)}) while((s32[]{:T(128)}, f32[1152,1152]{1,0:T(8,128)}, s32[9,2]{0,1:T(2,128)S(1)}, f32[9,128,128]{2,1,0:T(8,128)}, s32[]{:T(128)}) %tuple.112), condition=%wide.while_cond.4, body=%wide.while_body.4.sunk | while | flops 2 | bytes 132205 | solution.py:185
  623.5 2.9 bitcast_dynamic-update-slice_fusion.2
  627.0 2.9 bitcast_dynamic-update-slice_fusion.2
  630.5 2.9 bitcast_dynamic-update-slice_fusion.2
  634.0 2.9 bitcast_dynamic-update-slice_fusion.2
  637.5 2.9 bitcast_dynamic-update-slice_fusion.2
  641.0 2.9 bitcast_dynamic-update-slice_fusion.2
  644.5 2.9 bitcast_dynamic-update-slice_fusion.2
  648.0 2.9 bitcast_dynamic-update-slice_fusion.2
  651.4 2.8 bitcast_dynamic-update-slice_fusion.2
  654.3 90.0 %custom-call.84 = f32[9,128,128]{1,2,0:T(8,128)} custom-call(f32[9,128,128]{2,1,0:T(8,128)} %get-tuple-element.65), custom_call_target="InvertDiagBlocksLowerTriangular" | custom-call | tf_op jit(solution)/shard_map/triangular_solve | solution.py:185
  769.4 52.6 %all-reduce.24.cloned.1.call-done = (f32[288,128]{1,0:T(8,128)}, f32[288,128]{1,0:T(8,128)}) async-done(((f32[288,128]{1,0:T(8,128)}, f32[288,128]{1,0:T(8,128)}), (f32[288,128]{1,0:T(8,128)}, f32[288,128]{1,0:T(8,128)})) %all-reduce.24.cloned.1.call-update) | async-done | bytes 294928 | tf_op jit(solution)/shard_map/psum | solution.py:192
  825.1 11.2 %all_gather.19 = f32[1152,128]{1,0:T(8,128)S(1)} all-gather(f32[288,128]{1,0:T(8,128)S(1)} %get-tuple-element.128), channel_id=1, replica_groups=mesh['group'=1,'tile'=8,'dp'=4] {'dp'}, dimensions={0}, use_global_device_ids=true | all-gather | bytes 737280 | tf_op jit(solution)/shard_map/all_gather | solution.py:207
  (224 shorter events, 124.3 us)
Async XLA Ops:
  8.0 1.0 copy-start
  8.0 27.2 %copy-start.20 = (s32[4]{0:T(128)S(1)}, s32[4]{0:T(128)}, u32[]{:S(2)}) copy-start(s32[4]{0:T(128)} %constant.547.clone) | copy-start | bytes 52
  8.0 10.4 %copy-start.11 = (bf16[1,1,24,24,128]{4,3,2,1,0:T(8,128)(2,1)S(1)}, bf16[1,1,24,24,128]{4,3,2,1,0:T(8,128)(2,1)}, u32[]{:S(2)}) copy-start(bf16[1,1,24,24,128]{4,3,2,1,0:T(8,128)(2,1)} %param.20) | copy-start | bytes 442372
  8.0 27.0 %copy-start.19 = (s32[1,4]{1,0:T(1,128)S(1)}, s32[1,4]{1,0:T(1,128)}, u32[]{:S(2)}) copy-start(s32[1,4]{1,0:T(1,128)} %param.24) | copy-start | bytes 52
  8.1 189.4 %all-reduce.18.cloned.1.call-start = ((), (), s32[]{:S(2)}) async-start(), calls=%async_computation | async-start | bytes 1179648 | tf_op jit(solution)/shard_map/psum | solution.py:150
  18.3 252.2 %copy-start.13 = (f32[1,26,26,128]{3,2,1,0:T(8,128)}, f32[1,26,26,128]{3,2,1,0:T(8,128)S(1)}, u32[]{:S(2)}) copy-start(f32[1,26,26,128]{3,2,1,0:T(8,128)S(1)} %get-tuple-element.131) | copy-start | bytes 1038340
  18.3 35.3 %copy-start.14 = (f32[144,288]{1,0:T(8,128)S(1)}, f32[144,288]{1,0:T(8,128)}, u32[]{:S(2)}) copy-start(f32[144,288]{1,0:T(8,128)} %param.26) | copy-start | bytes 497668
  50.5 148.0 %copy-start.15 = (f32[144,1152]{1,0:T(8,128)S(1)}, f32[144,1152]{1,0:T(8,128)}, u32[]{:S(2)}) copy-start(f32[144,1152]{1,0:T(8,128)} %param.25) | copy-start | bytes 1990660
  51.0 1.1 copy-start.8
  53.6 145.8 %all-gather.4.cloned.1.call-start = ((), (), s32[]{:S(2)}) async-start(), calls=%async_computation.1 | async-start | bytes 2985984 | tf_op jit(solution)/shard_map/all_gather | solution.py:174
  65.2 204.1 %copy-start.18 = (f32[288,128]{1,0:T(8,128)S(1)}, f32[288,128]{1,0:T(8,128)}, u32[]{:S(2)}) copy-start(f32[288,128]{1,0:T(8,128)} %param.29) | copy-start | bytes 442372
  65.2 201.7 %all-reduce.20.cloned.1.call-start = ((), (), s32[]{:S(2)}) async-start(), calls=%async_computation.2 | async-start | bytes 2654208 | tf_op jit(solution)/shard_map/psum | solution.py:180
  198.6 566.7 %copy-start.5 = (f32[1152,128]{1,0:T(8,128)}, f32[1152,128]{1,0:T(8,128)S(1)}, u32[]{:S(2)}) copy-start(f32[1152,128]{1,0:T(8,128)S(1)} %broadcast_multiply_fusion) | copy-start | bytes 1769476
  199.3 72.0 %copy-start.9 = (f32[144,1152]{1,0:T(8,128)}, f32[144,1152]{1,0:T(8,128)S(1)}, u32[]{:S(2)}) copy-start(f32[144,1152]{1,0:T(8,128)S(1)} %fusion.1) | copy-start | bytes 1990660
  202.9 0.8 copy-start.6
  206.4 560.4 %all-reduce.22.cloned.1.call-start = ((), (), s32[]{:S(2)}) async-start(), calls=%async_computation.3 | async-start | bytes 147456 | tf_op jit(solution)/shard_map/psum | solution.py:190
  266.9 30.7 %collective-permute-start = (f32[1152,288]{0,1:T(8,128)}, f32[1152,288]{0,1:T(8,128)S(1)}, u32[]{:S(2)}, u32[]{:S(2)}) collective-permute-start(f32[1152,288]{0,1:T(8,128)} %all-reduce.20.cloned.1.call-done), channel_id=1, source_target_pairs={{0,3},{1,0},{2,1},{3,2},{4,7},{5,4},{6,5},{7,6},{8,11},{9,8},{10,9... | collective-permute-start | bytes 3981320 | tf_op jit(solution)/shard_map/ppermute | solution.py:16
  270.3 37.0 %copy-start.16 = (f32[128,128]{1,0:T(8,128)S(1)}, f32[128,128]{1,0:T(8,128)}, u32[]{:S(2)}) copy-start(f32[128,128]{1,0:T(8,128)} %param.28) | copy-start | bytes 196612
  270.3 551.7 %all-reduce.24.cloned.1.call-start = ((), (), s32[]{:S(2)}) async-start(), calls=%async_computation.4 | async-start | bytes 589824 | tf_op jit(solution)/shard_map/psum | solution.py:192
  271.3 64.9 %copy-start.4 = (f32[1152,288]{0,1:T(8,128)S(1)}, f32[1152,288]{0,1:T(8,128)}, u32[]{:S(2)}) copy-start(f32[1152,288]{0,1:T(8,128)} %all-reduce.20.cloned.1.call-done) | copy-start | bytes 3981316
  278.8 23.2 %copy-start.12 = (f32[1,24,24,128]{3,1,2,0:T(8,128)S(1)}, f32[1,24,24,128]{3,1,2,0:T(8,128)}, u32[]{:S(2)}) copy-start(f32[1,24,24,128]{3,1,2,0:T(8,128)} %fusion.136) | copy-start | bytes 884740
  300.6 58.7 %collective-permute-start.1 = (f32[1152,576]{0,1:T(8,128)}, f32[1152,576]{0,1:T(8,128)}, u32[]{:S(2)}, u32[]{:S(2)}) collective-permute-start(f32[1152,576]{0,1:T(8,128)} %pad_maximum_fusion), channel_id=1, source_target_pairs={{0,2},{1,3},{2,0},{3,1},{4,6},{5,7},{6,4},{7,5},{8,10},{9,11},{10,... | collective-permute-start | bytes 7962632 | tf_op jit(solution)/shard_map/ppermute | solution.py:16
  307.3 17.2 %copy-start.17 = (f32[128,128]{1,0:T(8,128)}, f32[128,128]{1,0:T(8,128)S(1)}, u32[]{:S(2)}) copy-start(f32[128,128]{1,0:T(8,128)S(1)} %fusion.11) | copy-start | bytes 196612
  363.3 4.0 copy-start.2
  381.9 2.3 copy-start.3
  617.6 126.7 %copy-start.7 = (f32[144,1152]{1,0:T(8,128)S(1)}, f32[144,1152]{1,0:T(8,128)}, u32[]{:S(2)}) copy-start(f32[144,1152]{1,0:T(8,128)} %copy-done.6) | copy-start | bytes 1990660
  753.6 84.3 %copy-start.1 = (bf16[1,1,24,24,128]{4,3,2,1,0:T(8,128)(2,1)S(1)}, bf16[1,1,24,24,128]{4,3,2,1,0:T(8,128)(2,1)}, u32[]{:S(2)}) copy-start(bf16[1,1,24,24,128]{4,3,2,1,0:T(8,128)(2,1)} %param.21) | copy-start | bytes 442372
  765.3 72.6 %copy-start.10 = (f32[1152,144]{0,1:T(8,128)}, f32[1152,144]{0,1:T(8,128)S(1)}, u32[]{:S(2)}) copy-start(f32[1152,144]{0,1:T(8,128)S(1)} %convolution_dynamic-update-slice_fusion.6) | copy-start | bytes 1990660
Sparse Core Ops, SparseCore 0:
  53.7 143.7 all-reduce.17
  270.4 58.9 all-reduce.21
Sparse Core Ops, SparseCore 1:
  65.3 35.0 all-gather.3
  206.4 60.4 all-reduce.19
  769.2 52.7 all-reduce.23
